TPU v7x, 32 devices: a whole 2x2x4 slice. The times are simulated.
32 devices in a mesh: dp: 8 (over z, core), seq: 4 (over y, x).
Axes of the slice: x: 2, y: 2, z: 4, core: 2. Of those that a mesh axis runs over, the one named last changes fastest.
Arguments:
- tokens_in: bfloat16 [16384, 1024], P(('dp', 'seq')), may hold values from -6 to 6
- norm_attn: bfloat16 [1024], P('dp'), may hold values from 0.5 to 1.5
- w_query: bfloat16 [1024, 1024], P('dp'), may hold values from -0.1875 to 0.1875
- key_value_weight: bfloat16 [1024, 1024], P('dp'), may hold values from -0.1875 to 0.1875
- gain_query: bfloat16 [64], P('dp'), may hold values from 1 to 2
- gain_key: bfloat16 [64], P('dp'), may hold values from 1 to 2
- w_out: bfloat16 [1024, 1024], P('dp'), may hold values from -0.75 to 0.75
- norm_ffn: bfloat16 [1024], P('dp'), may hold values from 0.5 to 1.5
- w_gate: bfloat16 [1024, 4608], P(None, 'dp'), may hold values from -0.1875 to 0.1875
- w_up: bfloat16 [1024, 4608], P(None, 'dp'), may hold values from -0.1875 to 0.1875
- w_down: bfloat16 [4608, 1024], P('dp'), may hold values from -0.09375 to 0.09375
- cotangent: bfloat16 [16384, 1024], P(('dp', 'seq')), may hold values from -6 to 6
- segments: int32 [8, 2048], P('dp'), may hold values from 0 to 3, never falling along the last dimension, each value on 1 to 1024 neighbouring positions
- blocks: int32 [8, 16], P('dp'), may hold values from 0 to 15, each once within a row
Outputs:
- output: bfloat16 [16384, 1024], P(('dp', 'seq'))
- grad_tokens: float32 [16384, 1024], P(('dp', 'seq'))
- grad_norm_attn: float32 [1024], P('dp')
- grad_w_query: float32 [1024, 1024], P('dp')
- grad_w_keyval: float32 [1024, 1024], P('dp')
- grad_gain_query: float32 [64], P('dp')
- grad_gain_key: float32 [64], P('dp')
- grad_w_out: float32 [1024, 1024], P('dp')
- grad_norm_ffn: float32 [1024], P('dp')
- grad_w_gate: float32 [1024, 4608], P(None, 'dp')
- grad_w_up: float32 [1024, 4608], P(None, 'dp')
- grad_w_down: float32 [4608, 1024], P('dp')
Inputs may be any that keep to these rules, and one draw needn't show every extreme that they name: `segments`: in each row the document numbers never fall, all 4 documents occur, each covers 1 to 1024 places and the longest exactly 1024. `blocks`: each row holds every block number once.
All inputs are finite; a program needn't handle non-finite values.
Results may differ from a plain program's by a relative error of at most 0.025.
Values may be sent and summed in bfloat16 or wider, within the bound.
A program may use at most 192 MiB of HBM per device.

v0:
```python
import math
import jax
import jax.numpy as jnp
from jax import lax
from jax.sharding import PartitionSpec as P

QUERY_HEADS = 16
KEY_VALUE_HEADS = 8
HEAD_SIZE = 64
BLOCK = 128
QUERY_ROWS = 512
EPS = 1e-05
THETA = 1000000.0
MASKED = -1e30


def normed(tensor, gain_vec):
    factor = lax.rsqrt(jnp.mean(tensor * tensor, axis=-1, keepdims=True) + EPS)
    return tensor * factor * gain_vec


def norm_back(tensor, gain_vec, upstream):
    factor = lax.rsqrt(jnp.mean(tensor * tensor, axis=-1, keepdims=True) + EPS)
    unit_value = tensor * factor
    weighted = upstream * gain_vec
    grad_in = factor * (
        weighted - unit_value * jnp.mean(weighted * unit_value, axis=-1, keepdims=True)
    )
    return (grad_in, upstream * unit_value)


def rotate(tensor, angle_cos, angle_sin):
    half_dim = tensor.shape[-1] // 2
    front_half = tensor[..., :half_dim]
    back_half = tensor[..., half_dim:]
    return jnp.concatenate(
        [
            front_half * angle_cos - back_half * angle_sin,
            back_half * angle_cos + front_half * angle_sin,
        ],
        axis=-1,
    )


def angles(offsets, head_dim):
    half_dim = head_dim // 2
    frequency = jnp.exp(
        jnp.arange(half_dim, dtype=jnp.float32) * (-2.0 * math.log(THETA) / head_dim)
    )
    turned = offsets.astype(jnp.float32)[:, None] * frequency[None, :]
    return (jnp.cos(turned)[:, None, :], jnp.sin(turned)[:, None, :])


def layout(segment_row, order_row, block_len):
    length_all = segment_row.shape[0]
    places = jnp.arange(length_all, dtype=jnp.int32)
    seg_start = jnp.concatenate([jnp.ones((1,), dtype=bool), segment_row[1:] != segment_row[:-1]])
    starts = lax.cummax(jnp.where(seg_start, places, 0), axis=0)
    offsets = places - starts
    placed_tokens = (
        order_row[:, None] * block_len + jnp.arange(block_len, dtype=jnp.int32)[None, :]
    ).reshape(length_all)
    return (placed_tokens, segment_row[placed_tokens], offsets[placed_tokens])


def plain_product(left_op, right_op):
    return jnp.dot(left_op, right_op, preferred_element_type=jnp.float32)


def dot_right_t(left_op, right_op):
    return lax.dot_general(
        left_op, right_op, (((1,), (1,)), ((), ())), preferred_element_type=jnp.float32
    )


def dot_left_t(left_op, right_op):
    return lax.dot_general(
        left_op, right_op, (((0,), (0,)), ((), ())), preferred_element_type=jnp.float32
    )


def gate_back(gate_pre, up_pre, upstream):
    gate_sig = jax.nn.sigmoid(gate_pre)
    grad_gate = upstream * up_pre * gate_sig * (1.0 + gate_pre * (1.0 - gate_sig))
    grad_up = upstream * gate_pre * gate_sig
    return (grad_gate.astype(jnp.bfloat16), grad_up.astype(jnp.bfloat16))


def shards(
    tokens_in,
    norm_attn,
    w_query,
    key_value_weight,
    gain_query,
    gain_key,
    w_out,
    norm_ffn,
    w_gate,
    w_up,
    w_down,
    cotangent,
    segments,
    blocks,
):
    sequence_count = lax.axis_size("seq")
    seq_index = lax.axis_index("seq")
    token_rows = tokens_in.shape[0]
    group_rows = token_rows * sequence_count
    local_key_value = KEY_VALUE_HEADS // sequence_count
    repeat_factor = QUERY_HEADS // KEY_VALUE_HEADS
    factor = HEAD_SIZE ** (-0.5)
    count_blocks = group_rows // QUERY_ROWS
    attn_gain, query_w, key_value_matrix, query_gain, key_gain, out_w, ffn_gain = (
        lax.all_gather(norm_attn, "dp", axis=0, tiled=True),
        lax.all_gather(w_query, "dp", axis=0, tiled=True),
        lax.all_gather(key_value_weight, "dp", axis=0, tiled=True),
        lax.all_gather(gain_query, "dp", axis=0, tiled=True),
        lax.all_gather(gain_key, "dp", axis=0, tiled=True),
        lax.all_gather(w_out, "dp", axis=0, tiled=True),
        lax.all_gather(norm_ffn, "dp", axis=0, tiled=True),
    )
    attn_gain = attn_gain.astype(jnp.float32)
    query_gain = query_gain.astype(jnp.float32)
    key_gain = key_gain.astype(jnp.float32)
    ffn_gain = ffn_gain.astype(jnp.float32)
    placed_tokens, documents_for_rows, offsets = layout(segments[0], blocks[0], BLOCK)
    angle_cos, angle_sin = angles(
        lax.dynamic_slice_in_dim(offsets, seq_index * token_rows, token_rows, 0), HEAD_SIZE
    )
    hidden = tokens_in.astype(jnp.float32)
    normalized_input = normed(hidden, attn_gain).astype(jnp.bfloat16)
    query_raw = plain_product(normalized_input, query_w).reshape(token_rows, QUERY_HEADS, HEAD_SIZE)
    key_value_unrotated = plain_product(normalized_input, key_value_matrix).reshape(
        token_rows, KEY_VALUE_HEADS, 2, HEAD_SIZE
    )
    query_low = rotate(normed(query_raw, query_gain), angle_cos, angle_sin).astype(jnp.bfloat16)
    key_low = rotate(normed(key_value_unrotated[:, :, 0], key_gain), angle_cos, angle_sin).astype(
        jnp.bfloat16
    )
    key_value_reduced = jnp.stack(
        [key_low, key_value_unrotated[:, :, 1].astype(jnp.bfloat16)], axis=2
    )
    query_heads, keyval_heads = (
        lax.all_to_all(
            query_low.reshape(token_rows, QUERY_HEADS * HEAD_SIZE),
            "seq",
            split_axis=1,
            concat_axis=0,
            tiled=True,
        ),
        lax.all_to_all(
            key_value_reduced.reshape(token_rows, KEY_VALUE_HEADS * 2 * HEAD_SIZE),
            "seq",
            split_axis=1,
            concat_axis=0,
            tiled=True,
        ),
    )
    query_matrix = query_heads.reshape(group_rows, local_key_value, repeat_factor, HEAD_SIZE)
    keyval_group = keyval_heads.reshape(group_rows, local_key_value, 2, HEAD_SIZE)
    key_rows = keyval_group[:, :, 0]
    value_rows = keyval_group[:, :, 1]

    def scores_of(block_idx):
        row_start = block_idx * QUERY_ROWS
        query_rows = lax.dynamic_slice_in_dim(query_matrix, row_start, QUERY_ROWS, 0)
        placed_rows = lax.dynamic_slice_in_dim(placed_tokens, row_start, QUERY_ROWS, 0)
        docs_rows = lax.dynamic_slice_in_dim(documents_for_rows, row_start, QUERY_ROWS, 0)
        allowed = (docs_rows[:, None] == documents_for_rows[None, :]) & (
            placed_tokens[None, :] <= placed_rows[:, None]
        )
        raw_scores = (
            jnp.einsum("rkad,jkd->karj", query_rows, key_rows, preferred_element_type=jnp.float32)
            * factor
        )
        return (query_rows, jnp.where(allowed, raw_scores, MASKED))

    def forward_block(block_idx):
        query_rows, masked = scores_of(block_idx)
        row_top = jnp.max(masked, axis=-1, keepdims=True)
        row_total = jnp.sum(jnp.exp(masked - row_top), axis=-1, keepdims=True)
        log_total = row_top + jnp.log(row_total)
        weights_low = jnp.exp(masked - log_total).astype(jnp.bfloat16)
        block_result = jnp.einsum(
            "karj,jkd->rkad", weights_low, value_rows, preferred_element_type=jnp.float32
        )
        return (block_result.astype(jnp.bfloat16), log_total)

    head_outs, log_totals = lax.map(forward_block, jnp.arange(count_blocks))
    attended = lax.all_to_all(
        head_outs.reshape(group_rows, local_key_value * repeat_factor * HEAD_SIZE),
        "seq",
        split_axis=0,
        concat_axis=1,
        tiled=True,
    )
    middle = hidden + plain_product(attended, out_w)
    ffn_in = normed(middle, ffn_gain).astype(jnp.bfloat16)
    gate_all, up_all, down_all = (
        lax.all_gather(w_gate, "dp", axis=1, tiled=True),
        lax.all_gather(w_up, "dp", axis=1, tiled=True),
        lax.all_gather(w_down, "dp", axis=0, tiled=True),
    )
    gate_pre = plain_product(ffn_in, gate_all)
    up_pre = plain_product(ffn_in, up_all)
    activated = (jax.nn.silu(gate_pre) * up_pre).astype(jnp.bfloat16)
    ffn_result = plain_product(activated, down_all)
    block_output = (middle + ffn_result).astype(jnp.bfloat16)
    upstream = cotangent.astype(jnp.float32)
    grad_act = dot_right_t(cotangent, down_all)
    grad_down_part = dot_left_t(activated, cotangent)
    grad_gate, grad_up = gate_back(gate_pre, up_pre, grad_act)
    grad_gate_part = dot_left_t(ffn_in, grad_gate)
    grad_up_part = dot_left_t(ffn_in, grad_up)
    grad_ffn_in = dot_right_t(grad_gate, gate_all) + dot_right_t(grad_up, up_all)
    grad_gate_w, grad_up_w, grad_down = (
        lax.psum_scatter(
            grad_gate_part.astype(jnp.bfloat16), "dp", scatter_dimension=1, tiled=True
        ).astype(jnp.float32),
        lax.psum_scatter(
            grad_up_part.astype(jnp.bfloat16), "dp", scatter_dimension=1, tiled=True
        ).astype(jnp.float32),
        lax.psum_scatter(
            grad_down_part.astype(jnp.bfloat16), "dp", scatter_dimension=0, tiled=True
        ).astype(jnp.float32),
    )
    grad_middle_add, ffn_gain_terms = norm_back(middle, ffn_gain, grad_ffn_in)
    grad_ffn_gain = jnp.sum(ffn_gain_terms, axis=0)
    grad_middle = upstream + grad_middle_add
    grad_branch = grad_middle.astype(jnp.bfloat16)
    grad_out_w = dot_left_t(attended, grad_branch)
    grad_attended = dot_right_t(grad_branch, out_w).astype(jnp.bfloat16)
    grad_head_outs = lax.all_to_all(grad_attended, "seq", split_axis=1, concat_axis=0, tiled=True)
    grad_outs_all = grad_head_outs.reshape(group_rows, local_key_value, repeat_factor, HEAD_SIZE)

    def backward_block(carried, group_members):
        grad_keys, grad_values = carried
        block_idx, log_total = group_members
        query_rows, masked = scores_of(block_idx)
        weights_full = jnp.exp(masked - log_total)
        weights_low = weights_full.astype(jnp.bfloat16)
        grad_rows = lax.dynamic_slice_in_dim(grad_outs_all, block_idx * QUERY_ROWS, QUERY_ROWS, 0)
        grad_weights = jnp.einsum(
            "rkad,jkd->karj", grad_rows, value_rows, preferred_element_type=jnp.float32
        )
        row_dot = jnp.sum(weights_full * grad_weights, axis=-1, keepdims=True)
        grad_scores = (weights_full * (grad_weights - row_dot)).astype(jnp.bfloat16)
        grad_query_rows = (
            jnp.einsum("karj,jkd->rkad", grad_scores, key_rows, preferred_element_type=jnp.float32)
            * factor
        )
        grad_keys = (
            grad_keys
            + jnp.einsum(
                "karj,rkad->jkd", grad_scores, query_rows, preferred_element_type=jnp.float32
            )
            * factor
        )
        grad_values = grad_values + jnp.einsum(
            "karj,rkad->jkd", weights_low, grad_rows, preferred_element_type=jnp.float32
        )
        return ((grad_keys, grad_values), grad_query_rows.astype(jnp.bfloat16))

    zero_heads = jnp.zeros((group_rows, local_key_value, HEAD_SIZE), jnp.float32)
    (grad_keys, grad_values), grad_query_blocks = lax.scan(
        backward_block, (zero_heads, zero_heads), (jnp.arange(count_blocks), log_totals)
    )
    grad_query_heads = grad_query_blocks.reshape(
        group_rows, local_key_value * repeat_factor * HEAD_SIZE
    )
    grad_keyval_heads = (
        jnp.stack([grad_keys, grad_values], axis=2)
        .astype(jnp.bfloat16)
        .reshape(group_rows, local_key_value * 2 * HEAD_SIZE)
    )
    grad_query_tok, key_value_gradient_tokens = (
        lax.all_to_all(grad_query_heads, "seq", split_axis=0, concat_axis=1, tiled=True),
        lax.all_to_all(grad_keyval_heads, "seq", split_axis=0, concat_axis=1, tiled=True),
    )
    grad_query_rot = rotate(
        grad_query_tok.reshape(token_rows, QUERY_HEADS, HEAD_SIZE).astype(jnp.float32),
        angle_cos,
        -angle_sin,
    )
    grad_query_raw, query_gain_terms = norm_back(query_raw, query_gain, grad_query_rot)
    grad_query_gain = jnp.sum(query_gain_terms, axis=(0, 1))
    key_value_gradient_split = key_value_gradient_tokens.reshape(
        token_rows, KEY_VALUE_HEADS, 2, HEAD_SIZE
    )
    grad_key_rot = rotate(
        key_value_gradient_split[:, :, 0].astype(jnp.float32), angle_cos, -angle_sin
    )
    grad_key_raw, key_gain_terms = norm_back(key_value_unrotated[:, :, 0], key_gain, grad_key_rot)
    grad_key_gain = jnp.sum(key_gain_terms, axis=(0, 1))
    grad_query_low = grad_query_raw.astype(jnp.bfloat16).reshape(
        token_rows, QUERY_HEADS * HEAD_SIZE
    )
    grad_keyval_low = jnp.stack(
        [grad_key_raw.astype(jnp.bfloat16), key_value_gradient_split[:, :, 1]], axis=2
    ).reshape(token_rows, KEY_VALUE_HEADS * 2 * HEAD_SIZE)
    grad_normed_in = dot_right_t(grad_query_low, query_w) + dot_right_t(
        grad_keyval_low, key_value_matrix
    )
    grad_query_w = dot_left_t(normalized_input, grad_query_low)
    grad_keyval_w = dot_left_t(normalized_input, grad_keyval_low)
    grad_hidden_add, attn_gain_terms = norm_back(hidden, attn_gain, grad_normed_in)
    grad_attn_gain = jnp.sum(attn_gain_terms, axis=0)
    grad_hidden = grad_middle + grad_hidden_add
    (
        owned_attn_gain,
        owned_query_w,
        owned_keyval_w,
        owned_query_gain,
        owned_key_gain,
        owned_out_w,
        owned_ffn_gain,
    ) = (
        lax.psum_scatter(
            grad_attn_gain.astype(jnp.bfloat16), "dp", scatter_dimension=0, tiled=True
        ).astype(jnp.float32),
        lax.psum_scatter(
            grad_query_w.astype(jnp.bfloat16), "dp", scatter_dimension=0, tiled=True
        ).astype(jnp.float32),
        lax.psum_scatter(
            grad_keyval_w.astype(jnp.bfloat16), "dp", scatter_dimension=0, tiled=True
        ).astype(jnp.float32),
        lax.psum_scatter(
            grad_query_gain.astype(jnp.bfloat16), "dp", scatter_dimension=0, tiled=True
        ).astype(jnp.float32),
        lax.psum_scatter(
            grad_key_gain.astype(jnp.bfloat16), "dp", scatter_dimension=0, tiled=True
        ).astype(jnp.float32),
        lax.psum_scatter(
            grad_out_w.astype(jnp.bfloat16), "dp", scatter_dimension=0, tiled=True
        ).astype(jnp.float32),
        lax.psum_scatter(
            grad_ffn_gain.astype(jnp.bfloat16), "dp", scatter_dimension=0, tiled=True
        ).astype(jnp.float32),
    )
    (
        total_attn_gain,
        total_query_w,
        total_keyval_w,
        total_query_gain,
        total_key_gain,
        total_out_w,
        total_ffn_gain,
        total_gate_w,
        total_up_w,
        total_down_w,
    ) = lax.psum(
        (
            owned_attn_gain,
            owned_query_w,
            owned_keyval_w,
            owned_query_gain,
            owned_key_gain,
            owned_out_w,
            owned_ffn_gain,
            grad_gate_w,
            grad_up_w,
            grad_down,
        ),
        "seq",
    )
    return (
        block_output,
        grad_hidden,
        total_attn_gain,
        total_query_w,
        total_keyval_w,
        total_query_gain,
        total_key_gain,
        total_out_w,
        total_ffn_gain,
        total_gate_w,
        total_up_w,
        total_down_w,
    )


def solution(mesh):
    return jax.shard_map(
        shards,
        mesh=mesh,
        in_specs=(
            P(("dp", "seq"), None),
            P("dp"),
            P("dp", None),
            P("dp", None),
            P("dp"),
            P("dp"),
            P("dp", None),
            P("dp"),
            P(None, "dp"),
            P(None, "dp"),
            P("dp", None),
            P(("dp", "seq"), None),
            P("dp", None),
            P("dp", None),
        ),
        out_specs=(
            P(("dp", "seq"), None),
            P(("dp", "seq"), None),
            P("dp"),
            P("dp", None),
            P("dp", None),
            P("dp"),
            P("dp"),
            P("dp", None),
            P("dp"),
            P(None, "dp"),
            P(None, "dp"),
            P("dp", None),
        ),
        check_vma=False,
    )
```

profile of v0, /device:TPU:8, one launch (start us, length us, event | category | flops | bytes accessed | tf_op | source)
XLA Modules:
  0.0 1338.1 jit_solution(3187364560856251971)
XLA Ops:
  22.0 14.6 %all-reduce.8 = (bf16[64]{0:T(256)(128)(2,1)S(1)}, bf16[64]{0:T(256)(128)(2,1)S(1)}) all-reduce(bf16[64]{0:T(256)(128)(2,1)S(1)} %dynamic-update-slice, bf16[64]{0:T(256)(128)(2,1)S(1)} %dynamic-update-slice.1), channel_id=1, replica_groups=mesh['dp'=8,'seq'=4] {'dp'}, use_global_device_ids=true, to_apply=%add | all-reduce | flops 128 | bytes 512
  37.3 11.8 gather_fusion.1
  80.3 11.8 gather_fusion
  102.5 61.7 %while.28 = (s32[]{:T(128)}, bf16[4,512,2,2,64]{1,4,3,2,0:T(8,128)(2,1)}, f32[4,2,2,512,1]{3,2,1,4,0:T(2,128)}, s32[4]{0:T(128)S(1)}, s32[2048]{0:T(1024)S(1)}, ...) while((s32[]{:T(128)}, ...), condition=%wide.region_8.9_spmd.clone, body=%wide.region_5.8_spmd.clone.sunk | while | flops 1123155968 | bytes 56201496 | solution.py:189
  168.6 12.5 all-gather.1
  199.9 80.6 %all-gather.17.cloned.1.call-done = bf16[1024,4608]{0,1:T(8,128)(2,1)} async-done(((bf16[1024,576]{0,1:T(8,128)(2,1)}), bf16[1024,4608]{0,1:T(8,128)(2,1)}) %all-gather.17.cloned.1.call-update) | async-done | bytes 9437200 | tf_op jit(solution)/shard_map/all_gather | solution.py:201
  290.7 80.5 %all-gather.19.cloned.1.call-done = bf16[4608,1024]{1,0:T(8,128)(2,1)} async-done(((bf16[576,1024]{1,0:T(8,128)(2,1)}), bf16[4608,1024]{1,0:T(8,128)(2,1)}) %all-gather.19.cloned.1.call-update) | async-done | bytes 9437200 | tf_op jit(solution)/shard_map/all_gather | solution.py:202
  371.2 18.5 %multiply_convert_fusion = (bf16[512,4608]{1,0:T(8,128)(2,1)}, bf16[512,4608]{1,0:T(8,128)(2,1)}, bf16[512,4608]{1,0:T(8,128)(2,1)}) fusion(f32[512,4608]{1,0:T(8,128)} %fusion.93, f32[512,4608]{1,0:T(8,128)} %fusion.94, bf16[512,1024]{1,0:T(8,128)(2,1)} %param.29, bf16[4608,1024]{1,0:T(8,128)(2,1)} %all-gather.19.cloned.1.call-done), kind=kOutput, calls=%fused_computation.69 | convolution fusion | flops 4869586944 | bytes 43515904 | tf_op jit(solution)/shard_map/dot_general | solution.py:71
  434.4 199.1 %while.29 = (s32[]{:T(128)}, f32[2048,2,64]{0,2,1:T(8,128)}, f32[2048,2,64]{0,2,1:T(8,128)}, bf16[4,512,2,2,64]{1,4,3,2,0:T(8,128)(2,1)}, s32[4]{0:T(128)S(1)}, ...) while((s32[]{:T(128)}, f32[2048,2,64]{0,2,1:T(8,128)}, ...), condition=%wide.region_13.14_spmd.clone, body=%wide.region_11.13_spmd.clone.sunk | while | flops 2751987712 | bytes 254768080 | solution.py:265
  442.1 11.6 fusion.160
  453.6 10.9 fusion.161
  491.6 11.5 fusion.160
  503.1 10.9 fusion.161
  541.3 11.5 fusion.160
  552.8 10.9 fusion.161
  591.0 11.5 fusion.160
  602.6 10.9 fusion.161
  639.4 11.2 all-to-all-done.4
  668.3 16.0 %all_to_all.90 = bf16[4,512,256]{1,2,0:T(8,128)(2,1)S(1)} all-to-all(bf16[4,512,256]{1,2,0:T(8,128)(2,1)S(1)} %copy.108), channel_id=1, replica_groups=mesh['dp'=8,'seq'=4] {'seq'}, dimensions={0} | all-to-all | bytes 2097152 | tf_op jit(solution)/shard_map/all_to_all | solution.py:278
  741.4 13.4 %all-reduce.7 = (bf16[1024]{0:T(1024)(128)(2,1)S(1)}, bf16[64]{0:T(256)(128)(2,1)S(1)}, bf16[64]{0:T(256)(128)(2,1)S(1)}, bf16[1024]{0:T(1024)(128)(2,1)S(1)}) all-reduce(bf16[1024]{0:T(1024)(128)(2,1)S(1)} %get-tuple-element.224, bf16[64]{0:T(256)(128)(2,1)S(1)} %reduce_sum.160, ...), channel_id=2, replica_groups=mesh['dp'=8,'seq'=4] {'dp'}, use_global_device_ids=true, to_apply=%region_18.19.clone | all-reduce | flops 2176 | bytes 8704
  758.6 78.1 %reduce-scatter.13.cloned.1.call-done = bf16[1024,576]{0,1:T(8,128)(2,1)} async-done(((bf16[1024,4608]{0,1:T(8,128)(2,1)}), bf16[1024,576]{0,1:T(8,128)(2,1)}) %reduce-scatter.13.cloned.1.call-update) | async-done | bytes 1179664 | tf_op jit(solution)/shard_map/reduce_scatter | solution.py:217
  836.7 99.8 %reduce-scatter.15.cloned.1.call-done = bf16[1024,576]{0,1:T(8,128)(2,1)} async-done(((bf16[1024,4608]{0,1:T(8,128)(2,1)}), bf16[1024,576]{0,1:T(8,128)(2,1)}) %reduce-scatter.15.cloned.1.call-update) | async-done | bytes 1179664 | tf_op jit(solution)/shard_map/reduce_scatter | solution.py:220
  936.5 100.1 %reduce-scatter.17.cloned.1.call-done = bf16[576,1024]{1,0:T(8,128)(2,1)} async-done(((bf16[4608,1024]{1,0:T(8,128)(2,1)}), bf16[576,1024]{1,0:T(8,128)(2,1)}) %reduce-scatter.17.cloned.1.call-update) | async-done | bytes 1179664 | tf_op jit(solution)/shard_map/reduce_scatter | solution.py:223
  1036.6 294.2 %all-reduce.10 = (f32[128]{0:T(128)}, f32[128,1024]{1,0:T(8,128)}, f32[128,1024]{1,0:T(8,128)}, f32[8]{0:T(128)}, f32[8]{0:T(128)}, /*index=5*/f32[128,1024]{1,0...) all-reduce(f32[128]{0:T(128)S(1)} %dynamic-slice_convert_fusion.4, ...), channel_id=1, replica_groups=mesh['dp'=8,'seq'=4] {'seq'}, use_global_device_ids=true, to_apply=%region_19.20 | all-reduce | flops 2162960 | bytes 12978304 | tf_op jit(solution)/shard_map/psum | solution.py:351
  (456 shorter events, 381.0 us)
Async XLA Ops:
  7.2 29.9 %copy-start.58 = (s32[1,16]{1,0:T(1,128)S(1)}, s32[1,16]{1,0:T(1,128)}, u32[]{:S(2)}) copy-start(s32[1,16]{1,0:T(1,128)} %param.31) | copy-start | bytes 196
  7.2 43.2 %all-gather.9.cloned.1.call-start = ((), (), s32[]{:S(2)}) async-start(), calls=%async_computation.12 | async-start | bytes 2359296 | tf_op jit(solution)/shard_map/all_gather | solution.py:115
  8.0 62.5 %all-gather.11.cloned.1.call-start = ((), (), s32[]{:S(2)}) async-start(), calls=%async_computation.13 | async-start | bytes 2359296 | tf_op jit(solution)/shard_map/all_gather | solution.py:116
  8.7 172.4 %all-gather.13.cloned.1.call-start = ((), (), s32[]{:S(2)}) async-start(), calls=%async_computation.14 | async-start | bytes 2359296 | tf_op jit(solution)/shard_map/all_gather | solution.py:119
  9.5 180.3 %all-gather.15.cloned.1.call-start = ((), (), s32[]{:S(2)}) async-start(), calls=%async_computation.15 | async-start | bytes 10616832 | tf_op jit(solution)/shard_map/all_gather | solution.py:200
  10.0 270.4 %all-gather.17.cloned.1.call-start = ((), (), s32[]{:S(2)}) async-start(), calls=%async_computation.16 | async-start | bytes 10616832 | tf_op jit(solution)/shard_map/all_gather | solution.py:201
  20.3 50.2 %copy-start.40 = (f32[8,1,128]{2,1,0:T(1,128)}, f32[8,1,128]{2,1,0:T(1,128)S(1)}, u32[]{:S(2)}) copy-start(f32[8,1,128]{2,1,0:T(1,128)S(1)} %convert_element_type.218) | copy-start | bytes 12292
  36.6 20.3 %copy-start.46 = (f32[64]{0:T(128)}, f32[64]{0:T(128)S(1)}, u32[]{:S(2)}) copy-start(f32[64]{0:T(128)S(1)} %convert_element_type.174) | copy-start | bytes 772
  36.7 37.1 %copy-start.44 = (f32[64]{0:T(128)}, f32[64]{0:T(128)S(1)}, u32[]{:S(2)}) copy-start(f32[64]{0:T(128)S(1)} %convert_element_type.177) | copy-start | bytes 772
  49.5 21.0 %copy-start.42 = (f32[512]{0:T(512)}, f32[512]{0:T(512)S(1)}, u32[]{:S(2)}) copy-start(f32[512]{0:T(512)S(1)} %add_rsqrt_fusion.3) | copy-start | bytes 6148
  50.4 24.4 %copy-start.21 = (f32[512,32]{0,1:T(8,128)}, f32[512,32]{0,1:T(8,128)S(1)}, u32[]{:S(2)}) copy-start(f32[512,32]{0,1:T(8,128)S(1)} %get-tuple-element.315) | copy-start | bytes 196612
  59.4 16.7 %all-to-all-start = ((bf16[512,4,256]{0,2,1:T(8,128)(2,1)}), bf16[512,4,256]{0,2,1:T(8,128)(2,1)S(1)}, u32[]{:S(2)}, u32[]{:S(2)}) async-start(bf16[512,4,256]{0,2,1:T(8,128)(2,1)} %bitcast.11), calls=%async_computation | async-start | bytes 2097152 | tf_op jit(solution)/shard_map/all_to_all | solution.py:144
  76.1 19.6 %all-to-all-start.1 = ((bf16[512,4,256]{0,2,1:T(8,128)(2,1)}), bf16[512,4,256]{0,2,1:T(8,128)(2,1)S(1)}, u32[]{:S(2)}, u32[]{:S(2)}) async-start(bf16[512,4,256]{0,2,1:T(8,128)(2,1)} %bitcast.17), calls=%async_computation.1 | async-start | bytes 2097152 | tf_op jit(solution)/shard_map/all_to_all | solution.py:151
  79.8 291.4 %all-gather.19.cloned.1.call-start = ((), (), s32[]{:S(2)}) async-start(), calls=%async_computation.17 | async-start | bytes 10616832 | tf_op jit(solution)/shard_map/all_gather | solution.py:202
  164.2 18.7 %all-to-all-start.2 = ((bf16[4,512,256]{1,2,0:T(8,128)(2,1)}), bf16[4,512,256]{1,2,0:T(8,128)(2,1)}, u32[]{:S(2)}, u32[]{:S(2)}) async-start(bf16[4,512,256]{1,2,0:T(8,128)(2,1)} %bitcast.312), calls=%async_computation.2 | async-start | bytes 2097152 | tf_op jit(solution)/shard_map/all_to_all | solution.py:190
  409.3 18.7 %all-to-all-start.3 = ((bf16[512,4,256]{2,0,1:T(8,128)(2,1)}), bf16[512,4,256]{2,0,1:T(8,128)(2,1)}, u32[]{:S(2)}, u32[]{:S(2)}) async-start(bf16[512,4,256]{2,0,1:T(8,128)(2,1)} %bitcast.310), calls=%async_computation.3 | async-start | bytes 2097152 | tf_op jit(solution)/shard_map/all_to_all | solution.py:233
  413.6 345.0 %reduce-scatter.11.cloned.1.call-start = ((), (), s32[]{:S(2)}) async-start(), calls=%async_computation.20 | async-start | bytes 2359296 | tf_op jit(solution)/shard_map/reduce_scatter | solution.py:333
  633.5 17.1 %all-to-all-start.4 = ((bf16[4,512,256]{1,2,0:T(8,128)(2,1)}), bf16[4,512,256]{1,2,0:T(8,128)(2,1)S(1)}, u32[]{:S(2)}, u32[]{:S(2)}) async-start(bf16[4,512,256]{1,2,0:T(8,128)(2,1)} %bitcast.311), calls=%async_computation.4 | async-start | bytes 2097152 | tf_op jit(solution)/shard_map/all_to_all | solution.py:277
  637.1 121.5 %reduce-scatter.7.cloned.1.call-start = ((), (), s32[]{:S(2)}) async-start(), calls=%async_computation.18 | async-start | bytes 2359296 | tf_op jit(solution)/shard_map/reduce_scatter | solution.py:321
  665.5 93.1 %reduce-scatter.9.cloned.1.call-start = ((), (), s32[]{:S(2)}) async-start(), calls=%async_computation.19 | async-start | bytes 2359296 | tf_op jit(solution)/shard_map/reduce_scatter | solution.py:324
  690.7 146.0 %reduce-scatter.13.cloned.1.call-start = ((), (), s32[]{:S(2)}) async-start(), calls=%async_computation.21 | async-start | bytes 10616832 | tf_op jit(solution)/shard_map/reduce_scatter | solution.py:217
  702.0 234.6 %reduce-scatter.15.cloned.1.call-start = ((), (), s32[]{:S(2)}) async-start(), calls=%async_computation.22 | async-start | bytes 10616832 | tf_op jit(solution)/shard_map/reduce_scatter | solution.py:220
  712.2 324.4 %reduce-scatter.17.cloned.1.call-start = ((), (), s32[]{:S(2)}) async-start(), calls=%async_computation.23 | async-start | bytes 10616832 | tf_op jit(solution)/shard_map/reduce_scatter | solution.py:223
  738.4 16.8 %copy-start.19 = (f32[512,1024]{1,0:T(8,128)S(1)}, f32[512,1024]{1,0:T(8,128)}, u32[]{:S(2)}) copy-start(f32[512,1024]{1,0:T(8,128)} %copy-done.18) | copy-start | bytes 6291460
  (108 other events, 590.8 us)
Sparse Core Ops, SparseCore 0:
  9.7 30.5 all-gather.8
  41.9 28.5 all-gather.10
  72.1 28.5 all-gather.12
  102.2 87.5 all-gather.14
  191.3 89.1 all-gather.16
  282.0 89.1 all-gather.18
  418.3 33.8 reduce-scatter.10
  665.7 32.2 reduce-scatter.6
  700.3 34.5 reduce-scatter.8
  737.0 99.7 reduce-scatter.12
  839.0 97.4 reduce-scatter.14
  938.7 97.8 reduce-scatter.16
where the time goes:
time: 1350 us; the launch traced here: 1340 us
  waiting for transfers between devices  474 us (35%)
  blocking collectives  360 us (27%)
  matrix products  293 us (22%)
  other arithmetic  94.1 us (7%)
  local copies, waits for them, and re-layouts  73.3 us (5%)
  starting transfers between devices  20.2 us (1%)
  between operations  17.5 us (1%)
    psum x1, blocking collectives, shards(): lax.psum((owned_attn_gain, owned_query_w, owned_keyval_w, owned_query_gai...  294 us
    reduce_scatter x1, waiting for transfers between devices, shards(): lax.psum_scatter(grad_down_part.astype(jnp.bfloat16), 'dp', scatter_dimen...  100 us
    reduce_scatter x1, waiting for transfers between devices, shards(): lax.psum_scatter(grad_up_part.astype(jnp.bfloat16), 'dp', scatter_dimensi...  99.8 us
    all_gather x1, waiting for transfers between devices, shards(): lax.all_gather(w_up, 'dp', axis=1, tiled=True)  80.6 us
    all_gather x1, waiting for transfers between devices, shards(): lax.all_gather(w_down, 'dp', axis=0, tiled=True)  80.5 us
    reduce_scatter x1, waiting for transfers between devices, shards(): lax.psum_scatter(grad_gate_part.astype(jnp.bfloat16), 'dp', scatter_dimen...  78.1 us
    dot_general x4, matrix products, backward_block(): jnp.einsum('rkad,jkd->karj', grad_rows, value_rows, preferred_element_typ...  46.1 us
    convert_element_type x4, other arithmetic, backward_block(): grad_scores = (weights_full * (grad_weights - row_dot)).astype(jnp.bfloat16)  43.6 us
  transfers between devices with their start and end apart: 17, of which 10 were waited for; matrix products, arithmetic and copies ran while one was open for 31% of the time, Pallas kernels for 0%

commit v1 on v0

--- a/solution.py
+++ b/solution.py
@@ -12,6 +12,28 @@
 EPS = 1e-05
 THETA = 1000000.0
 MASKED = -1e30
+
+
+def in_order(blocks, dim):
+    dims = list(blocks.shape[1:])
+    dims[dim] *= blocks.shape[0]
+    return jnp.moveaxis(blocks, 0, dim).reshape(dims)
+
+
+def ring_gather(shard, axis, dim):
+    peers = lax.axis_size(axis)
+    pairs = [(i, (i + 1) % peers) for i in range(peers)]
+    back = [(b, a) for a, b in pairs]
+    lower, upper = ([], [])
+    for step in range(peers - 1):
+        if step % 2 == 0:
+            lower.append(lax.ppermute(lower[-1] if lower else shard, axis, pairs))
+        else:
+            upper.append(lax.ppermute(upper[-1] if upper else shard, axis, back))
+    blocks = jnp.stack([*lower[::-1], shard, *upper])
+    shift = lax.axis_index(axis) - len(lower)
+    blocks = blocks[(jnp.arange(peers) - shift) % peers]
+    return in_order(blocks, dim)
 
 
 def normed(tensor, gain_vec):
@@ -198,7 +220,7 @@
     ffn_in = normed(middle, ffn_gain).astype(jnp.bfloat16)
     gate_all, up_all, down_all = (
         lax.all_gather(w_gate, "dp", axis=1, tiled=True),
-        lax.all_gather(w_up, "dp", axis=1, tiled=True),
+        ring_gather(w_up, "dp", 1),
         lax.all_gather(w_down, "dp", axis=0, tiled=True),
     )
     gate_pre = plain_product(ffn_in, gate_all)

time: 1350 us -> 1330 us (0.985)
  waiting for transfers between devices: 474 us -> 377 us
  blocking collectives: 360 us -> 401 us
  local copies, waits for them, and re-layouts: 73.3 us -> 99.3 us
    all_gather x1 -> x0, waiting for transfers between devices: 80.6 us -> none  [shards(): lax.all_gather(w_up, 'dp', axis=1, tiled=True)]
    all_gather x1, waiting for transfers between devices: 80.5 us -> 0.01 us  [shards(): lax.all_gather(w_down, 'dp', axis=0, tiled=True)]
    all_gather x1, waiting for transfers between devices: 0.82 us -> 60.5 us  [shards(): lax.all_gather(w_gate, 'dp', axis=1, tiled=True)]
    all_gather x1, blocking collectives: 9 us -> 46.3 us  [shards(): lax.all_gather(norm_attn, 'dp', axis=0, tiled=True)]
    unnamed x99 -> x108, local copies, waits for them, and re-layouts: 12.5 us -> 26.9 us
  transfers between devices with their start and end apart: 17 -> 23, of which waited for: 10 -> 8; matrix products, arithmetic and copies ran while one was open for 31% -> 33% of each run, Pallas kernels for 0% -> 0%
where the time goes in v1:
time: 1330 us; the launch traced here: 1320 us
  blocking collectives  401 us (30%)
  waiting for transfers between devices  377 us (28%)
  matrix products  295 us (22%)
  local copies, waits for them, and re-layouts  99.3 us (7%)
  other arithmetic  94.6 us (7%)
  starting transfers between devices  26 us (2%)
  between operations  17.3 us (1%)
    psum x1, blocking collectives, shards(): lax.psum((owned_attn_gain, owned_query_w, owned_keyval_w, owned_query_gai...  294 us
    reduce_scatter x1, waiting for transfers between devices, shards(): lax.psum_scatter(grad_down_part.astype(jnp.bfloat16), 'dp', scatter_dimen...  100 us
    reduce_scatter x1, waiting for transfers between devices, shards(): lax.psum_scatter(grad_up_part.astype(jnp.bfloat16), 'dp', scatter_dimensi...  99.7 us
    reduce_scatter x1, waiting for transfers between devices, shards(): lax.psum_scatter(grad_gate_part.astype(jnp.bfloat16), 'dp', scatter_dimen...  78.1 us
    all_gather x1, waiting for transfers between devices, shards(): lax.all_gather(w_gate, 'dp', axis=1, tiled=True)  60.5 us
    dot_general x6, matrix products, plain_product(): return jnp.dot(left_op, right_op, preferred_element_type=jnp.float32)  48.9 us
    all_gather x1, blocking collectives, shards(): lax.all_gather(norm_attn, 'dp', axis=0, tiled=True)  46.3 us
    dot_general x4, matrix products, backward_block(): jnp.einsum('rkad,jkd->karj', grad_rows, value_rows, preferred_element_typ...  46.3 us
  transfers between devices with their start and end apart: 23, of which 8 were waited for; matrix products, arithmetic and copies ran while one was open for 33% of the time, Pallas kernels for 0%

profile of v1, /device:TPU:8, one launch (start us, length us, event | category | flops | bytes accessed | tf_op | source)
XLA Modules:
  0.0 1316.9 jit_solution(18358723241596488981)
XLA Ops:
  13.2 46.3 %all-gather = bf16[8,1,128]{2,1,0:T(2,128)(2,1)S(1)} all-gather(bf16[1,1,128]{2,1,0:T(2,128)(2,1)} %bitcast.352), channel_id=1, replica_groups=mesh['dp'=8,'seq'=4] {'dp'}, dimensions={0}, use_global_device_ids=true | all-gather | bytes 2304 | tf_op jit(solution)/shard_map/all_gather | solution.py:136
  61.3 12.8 all-reduce.8
  74.9 11.8 gather_fusion.1
  128.0 11.8 gather_fusion
  139.8 18.3 %all-gather.1 = bf16[8,1,128]{2,1,0:T(2,128)(2,1)S(1)} all-gather(bf16[1,1,128]{2,1,0:T(2,128)(2,1)S(1)} %bitcast.353), channel_id=1, replica_groups=mesh['dp'=8,'seq'=4] {'dp'}, dimensions={0}, use_global_device_ids=true | all-gather | bytes 2304 | tf_op jit(solution)/shard_map/all_gather | solution.py:142
  169.3 61.7 %while.28 = (s32[]{:T(128)}, bf16[4,512,2,2,64]{1,4,3,2,0:T(8,128)(2,1)}, f32[4,2,2,512,1]{3,2,1,4,0:T(2,128)}, s32[4]{0:T(128)S(1)}, s32[2048]{0:T(1024)S(1)}, ...) while((s32[]{:T(128)}, ...), condition=%wide.region_8.9_spmd.clone, body=%wide.region_5.8_spmd.clone.sunk | while | flops 1123155968 | bytes 56201496 | solution.py:211
  278.3 60.5 %all-gather.14.cloned.1.call-done = bf16[1024,4608]{0,1:T(8,128)(2,1)} async-done(((bf16[1024,576]{0,1:T(8,128)(2,1)}), bf16[1024,4608]{0,1:T(8,128)(2,1)}) %all-gather.14.cloned.1.call-update) | async-done | bytes 9437200 | tf_op jit(solution)/shard_map/all_gather | solution.py:222
  348.9 18.1 %multiply_convert_fusion = (bf16[512,4608]{1,0:T(8,128)(2,1)}, bf16[512,4608]{1,0:T(8,128)(2,1)}, bf16[512,4608]{1,0:T(8,128)(2,1)}) fusion(f32[512,4608]{1,0:T(8,128)} %fusion.96, f32[512,4608]{1,0:T(8,128)} %fusion.95, bf16[512,1024]{1,0:T(8,128)(2,1)} %multiply_convert_fusion.4, bf16[1024,4608]{0,1:T(8,128)(2,1)} %bitcast.318), kind=kOutput, calls=%fused_computation.70 | convolution fusion | flops 4869586944 | bytes 43515904 | tf_op jit(solution)/shard_map/dot_general | solution.py:89
  413.9 198.7 %while.29 = (s32[]{:T(128)}, f32[2048,2,64]{0,2,1:T(8,128)}, f32[2048,2,64]{0,2,1:T(8,128)}, bf16[4,512,2,2,64]{1,4,3,2,0:T(8,128)(2,1)}, s32[4]{0:T(128)S(1)}, ...) while((s32[]{:T(128)}, f32[2048,2,64]{0,2,1:T(8,128)}, ...), condition=%wide.region_13.14_spmd.clone, body=%wide.region_11.13_spmd.clone.sunk | while | flops 2751987712 | bytes 254768080 | solution.py:287
  421.5 11.6 fusion.162
  433.1 10.8 fusion.163
  470.9 11.6 fusion.162
  482.5 10.8 fusion.163
  520.5 11.6 fusion.162
  532.1 10.8 fusion.163
  570.2 11.6 fusion.162
  581.7 10.8 fusion.163
  618.5 11.2 all-to-all-done.4
  647.5 16.0 %all_to_all.90 = bf16[4,512,256]{1,2,0:T(8,128)(2,1)S(1)} all-to-all(bf16[4,512,256]{1,2,0:T(8,128)(2,1)S(1)} %copy.108), channel_id=1, replica_groups=mesh['dp'=8,'seq'=4] {'seq'}, dimensions={0} | all-to-all | bytes 2097152 | tf_op jit(solution)/shard_map/all_to_all | solution.py:300
  720.6 13.4 %all-reduce.7 = (bf16[1024]{0:T(1024)(128)(2,1)S(1)}, bf16[64]{0:T(256)(128)(2,1)S(1)}, bf16[64]{0:T(256)(128)(2,1)S(1)}, bf16[1024]{0:T(1024)(128)(2,1)S(1)}) all-reduce(bf16[1024]{0:T(1024)(128)(2,1)S(1)} %get-tuple-element.224, bf16[64]{0:T(256)(128)(2,1)S(1)} %reduce_sum.160, ...), channel_id=2, replica_groups=mesh['dp'=8,'seq'=4] {'dp'}, use_global_device_ids=true, to_apply=%region_18.19.clone | all-reduce | flops 2176 | bytes 8704
  737.7 78.1 %reduce-scatter.13.cloned.1.call-done = bf16[1024,576]{0,1:T(8,128)(2,1)} async-done(((bf16[1024,4608]{0,1:T(8,128)(2,1)}), bf16[1024,576]{0,1:T(8,128)(2,1)}) %reduce-scatter.13.cloned.1.call-update) | async-done | bytes 1179664 | tf_op jit(solution)/shard_map/reduce_scatter | solution.py:239
  815.9 99.7 %reduce-scatter.15.cloned.1.call-done = bf16[1024,576]{0,1:T(8,128)(2,1)} async-done(((bf16[1024,4608]{0,1:T(8,128)(2,1)}), bf16[1024,576]{0,1:T(8,128)(2,1)}) %reduce-scatter.15.cloned.1.call-update) | async-done | bytes 1179664 | tf_op jit(solution)/shard_map/reduce_scatter | solution.py:242
  915.5 100.2 %reduce-scatter.17.cloned.1.call-done = bf16[576,1024]{1,0:T(8,128)(2,1)} async-done(((bf16[4608,1024]{1,0:T(8,128)(2,1)}), bf16[576,1024]{1,0:T(8,128)(2,1)}) %reduce-scatter.17.cloned.1.call-update) | async-done | bytes 1179664 | tf_op jit(solution)/shard_map/reduce_scatter | solution.py:245
  1015.7 294.2 %all-reduce.10 = (f32[128]{0:T(128)}, f32[128,1024]{1,0:T(8,128)}, f32[128,1024]{1,0:T(8,128)}, f32[8]{0:T(128)}, f32[8]{0:T(128)}, /*index=5*/f32[128,1024]{1,0...) all-reduce(f32[128]{0:T(128)S(1)} %dynamic-slice_convert_fusion.4, ...), channel_id=1, replica_groups=mesh['dp'=8,'seq'=4] {'seq'}, use_global_device_ids=true, to_apply=%region_19.20 | all-reduce | flops 2162960 | bytes 12978304 | tf_op jit(solution)/shard_map/psum | solution.py:373
  (480 shorter events, 410.9 us)
Async XLA Ops:
  7.2 67.4 %copy-start.59 = (s32[1,16]{1,0:T(1,128)S(1)}, s32[1,16]{1,0:T(1,128)}, u32[]{:S(2)}) copy-start(s32[1,16]{1,0:T(1,128)} %param.31) | copy-start | bytes 196
  7.2 88.9 %all-gather.8.cloned.1.call-start = ((), (), s32[]{:S(2)}) async-start(), calls=%async_computation.12 | async-start | bytes 2359296 | tf_op jit(solution)/shard_map/all_gather | solution.py:137
  8.0 101.1 %all-gather.10.cloned.1.call-start = ((), (), s32[]{:S(2)}) async-start(), calls=%async_computation.13 | async-start | bytes 2359296 | tf_op jit(solution)/shard_map/all_gather | solution.py:138
  8.7 253.4 %all-gather.12.cloned.1.call-start = ((), (), s32[]{:S(2)}) async-start(), calls=%async_computation.14 | async-start | bytes 2359296 | tf_op jit(solution)/shard_map/all_gather | solution.py:141
  9.4 258.7 %all-gather.16.cloned.1.call-start = ((), (), s32[]{:S(2)}) async-start(), calls=%async_computation.16 | async-start | bytes 10616832 | tf_op jit(solution)/shard_map/all_gather | solution.py:224
  10.0 64.6 %collective-permute-start = (bf16[1024,576]{0,1:T(8,128)(2,1)}, bf16[1024,576]{0,1:T(8,128)(2,1)S(1)}, u32[]{:S(2)}, u32[]{:S(2)}) collective-permute-start(bf16[1024,576]{0,1:T(8,128)(2,1)} %param.27), channel_id=1, source_target_pairs={{0,4},{4,8},{8,12},{12,16},{16,20},{20,24},{24,28},{28,0},{1,5},{5... | collective-permute-start | bytes 3538952 | tf_op jit(solution)/shard_map/ppermute | solution.py:30
  10.1 78.0 %collective-permute-start.4 = (bf16[1024,576]{0,1:T(8,128)(2,1)}, bf16[1024,576]{0,1:T(8,128)(2,1)}, u32[]{:S(2)}, u32[]{:S(2)}) collective-permute-start(bf16[1024,576]{0,1:T(8,128)(2,1)} %param.27), channel_id=1, source_target_pairs={{4,0},{8,4},{12,8},{16,12},{20,16},{24,20},{28,24},{0,28},{5,1},{9... | collective-permute-start | bytes 3538952 | tf_op jit(solution)/shard_map/ppermute | solution.py:32
  74.7 21.4 %collective-permute-start.1 = (bf16[1024,576]{0,1:T(8,128)(2,1)S(1)}, bf16[1024,576]{0,1:T(8,128)(2,1)}, u32[]{:S(2)}, u32[]{:S(2)}) collective-permute-start(bf16[1024,576]{0,1:T(8,128)(2,1)S(1)} %collective-permute-done), channel_id=1, source_target_pairs={{0,4},{4,8},{8,12},{12,16},{16,20},{20,24},{24,28},{28,0},{1,5},{5... | collective-permute-start | bytes 3538952 | tf_op jit(solution)/shard_map/ppermute | solution.py:30
  88.1 70.1 %collective-permute-start.5 = (bf16[1024,576]{0,1:T(8,128)(2,1)}, bf16[1024,576]{0,1:T(8,128)(2,1)}, u32[]{:S(2)}, u32[]{:S(2)}) collective-permute-start(bf16[1024,576]{0,1:T(8,128)(2,1)} %collective-permute-done.4), channel_id=1, source_target_pairs={{4,0},{8,4},{12,8},{16,12},{20,16},{24,20},{28,24},{0,28},{5,1},{9... | collective-permute-start | bytes 3538952 | tf_op jit(solution)/shard_map/ppermute | solution.py:32
  96.1 62.1 %collective-permute-start.2 = (bf16[1024,576]{0,1:T(8,128)(2,1)}, bf16[1024,576]{0,1:T(8,128)(2,1)}, u32[]{:S(2)}, u32[]{:S(2)}) collective-permute-start(bf16[1024,576]{0,1:T(8,128)(2,1)} %collective-permute-done.1), channel_id=1, source_target_pairs={{0,4},{4,8},{8,12},{12,16},{16,20},{20,24},{24,28},{28,0},{1,5},{5... | collective-permute-start | bytes 3538952 | tf_op jit(solution)/shard_map/ppermute | solution.py:30
  105.0 18.8 %all-to-all-start = ((bf16[512,4,256]{0,2,1:T(8,128)(2,1)}), bf16[512,4,256]{0,2,1:T(8,128)(2,1)S(1)}, u32[]{:S(2)}, u32[]{:S(2)}) async-start(bf16[512,4,256]{0,2,1:T(8,128)(2,1)} %bitcast.333), calls=%async_computation | async-start | bytes 2097152 | tf_op jit(solution)/shard_map/all_to_all | solution.py:166
  123.8 38.7 %all-to-all-start.1 = ((bf16[512,4,256]{0,2,1:T(8,128)(2,1)}), bf16[512,4,256]{0,2,1:T(8,128)(2,1)S(1)}, u32[]{:S(2)}, u32[]{:S(2)}) async-start(bf16[512,4,256]{0,2,1:T(8,128)(2,1)} %bitcast.17), calls=%async_computation.1 | async-start | bytes 2097152 | tf_op jit(solution)/shard_map/all_to_all | solution.py:173
  127.4 211.5 %all-gather.14.cloned.1.call-start = ((), (), s32[]{:S(2)}) async-start(), calls=%async_computation.15 | async-start | bytes 10616832 | tf_op jit(solution)/shard_map/all_gather | solution.py:222
  158.2 92.0 %collective-permute-start.6 = (bf16[1024,576]{0,1:T(8,128)(2,1)}, bf16[1024,576]{0,1:T(8,128)(2,1)}, u32[]{:S(2)}, u32[]{:S(2)}) collective-permute-start(bf16[1024,576]{0,1:T(8,128)(2,1)} %collective-permute-done.5), channel_id=1, source_target_pairs={{4,0},{8,4},{12,8},{16,12},{20,16},{24,20},{28,24},{0,28},{5,1},{9... | collective-permute-start | bytes 3538952 | tf_op jit(solution)/shard_map/ppermute | solution.py:32
  158.2 77.5 %collective-permute-start.3 = (bf16[1024,576]{0,1:T(8,128)(2,1)}, bf16[1024,576]{0,1:T(8,128)(2,1)}, u32[]{:S(2)}, u32[]{:S(2)}) collective-permute-start(bf16[1024,576]{0,1:T(8,128)(2,1)} %collective-permute-done.2), channel_id=1, source_target_pairs={{0,4},{4,8},{8,12},{12,16},{16,20},{20,24},{24,28},{28,0},{1,5},{5... | collective-permute-start | bytes 3538952 | tf_op jit(solution)/shard_map/ppermute | solution.py:30
  231.0 31.1 %all-to-all-start.2 = ((bf16[4,512,256]{1,2,0:T(8,128)(2,1)}), bf16[4,512,256]{1,2,0:T(8,128)(2,1)}, u32[]{:S(2)}, u32[]{:S(2)}) async-start(bf16[4,512,256]{1,2,0:T(8,128)(2,1)} %bitcast.336), calls=%async_computation.2 | async-start | bytes 2097152 | tf_op jit(solution)/shard_map/all_to_all | solution.py:212
  388.9 18.6 %all-to-all-start.3 = ((bf16[512,4,256]{2,0,1:T(8,128)(2,1)}), bf16[512,4,256]{2,0,1:T(8,128)(2,1)}, u32[]{:S(2)}, u32[]{:S(2)}) async-start(bf16[512,4,256]{2,0,1:T(8,128)(2,1)} %bitcast.334), calls=%async_computation.3 | async-start | bytes 2097152 | tf_op jit(solution)/shard_map/all_to_all | solution.py:255
  393.2 344.6 %reduce-scatter.11.cloned.1.call-start = ((), (), s32[]{:S(2)}) async-start(), calls=%async_computation.19 | async-start | bytes 2359296 | tf_op jit(solution)/shard_map/reduce_scatter | solution.py:355
  612.6 17.1 %all-to-all-start.4 = ((bf16[4,512,256]{1,2,0:T(8,128)(2,1)}), bf16[4,512,256]{1,2,0:T(8,128)(2,1)S(1)}, u32[]{:S(2)}, u32[]{:S(2)}) async-start(bf16[4,512,256]{1,2,0:T(8,128)(2,1)} %bitcast.335), calls=%async_computation.4 | async-start | bytes 2097152 | tf_op jit(solution)/shard_map/all_to_all | solution.py:299
  616.3 121.5 %reduce-scatter.7.cloned.1.call-start = ((), (), s32[]{:S(2)}) async-start(), calls=%async_computation.17 | async-start | bytes 2359296 | tf_op jit(solution)/shard_map/reduce_scatter | solution.py:343
  644.6 93.1 %reduce-scatter.9.cloned.1.call-start = ((), (), s32[]{:S(2)}) async-start(), calls=%async_computation.18 | async-start | bytes 2359296 | tf_op jit(solution)/shard_map/reduce_scatter | solution.py:346
  669.9 146.0 %reduce-scatter.13.cloned.1.call-start = ((), (), s32[]{:S(2)}) async-start(), calls=%async_computation.20 | async-start | bytes 10616832 | tf_op jit(solution)/shard_map/reduce_scatter | solution.py:239
  681.1 234.4 %reduce-scatter.15.cloned.1.call-start = ((), (), s32[]{:S(2)}) async-start(), calls=%async_computation.21 | async-start | bytes 10616832 | tf_op jit(solution)/shard_map/reduce_scatter | solution.py:242
  691.4 324.4 %reduce-scatter.17.cloned.1.call-start = ((), (), s32[]{:S(2)}) async-start(), calls=%async_computation.22 | async-start | bytes 10616832 | tf_op jit(solution)/shard_map/reduce_scatter | solution.py:245
  (115 other events, 911.8 us)
Sparse Core Ops, SparseCore 0:
  9.7 45.3 all-gather.7
  56.6 31.4 all-gather.9
  89.8 44.1 all-gather.11
  135.5 112.6 all-gather.15
  249.7 89.1 all-gather.13
  397.9 33.7 reduce-scatter.10
  644.8 32.2 reduce-scatter.6
  679.3 34.6 reduce-scatter.8
  716.3 99.5 reduce-scatter.12
  818.0 97.4 reduce-scatter.14
  917.8 97.8 reduce-scatter.16
